TPU v7x, 256 devices: a whole 4x4x8 slice. The times are simulated.
256 devices in a mesh: ctx: 32 (over z, x), exp: 8 (over y, core).
Axes of the slice: x: 4, y: 4, z: 8, core: 2. Of those that a mesh axis runs over, the one named last changes fastest.
Arguments:
- grad_out: bfloat16 [32768, 2880], P(('ctx', 'exp')), may hold values from -6 to 6
- top_logits: float32 [32768, 4], P(('ctx', 'exp')), may hold values from -8 to 308
- expert_ids: int32 [32768, 4], P(('ctx', 'exp')), may hold values from 0 to 7, all different within a row; in each aligned block of 128 rows (0 to 127, 128 to 255, ...) at most 96 rows name the same one
- saved_hidden: bfloat16 [32, 8, 768, 1536], P('ctx', 'exp'), may hold values from -0.29882812 to 0.29882812
- w_down: bfloat16 [8, 1536, 2880], P('exp', 'ctx'), may hold values from -0.15625 to 0.15625
Outputs:
- logit_grad: float32 [32768, 4], P(('ctx', 'exp'))
- hidden_grad: bfloat16 [32, 8, 768, 1536], P('ctx', 'exp')
- down_grad: float32 [8, 1536, 2880], P('exp', 'ctx')
Inputs may be any that keep to these rules, and one draw needn't show every extreme that they name: `expert_ids`: each row names 4 different experts; among the rows of one device no expert is named by more than 96 rows, a bound that some blocks reach.
All inputs are finite; a program needn't handle non-finite values.
Results may differ from a plain program's by a relative error of at most 0.0048.
Values may be sent and summed in bfloat16 or wider, within the bound.
A program may use at most 128 MiB of HBM per device.

v0:
```python
import jax
import jax.numpy as jnp
from jax import lax
from jax.sharding import PartitionSpec as P


def routing_tables(expert_ids, count_experts, capacity):
    columns = jnp.arange(count_experts, dtype=jnp.int32)
    matches = expert_ids[:, :, None] == columns[None, None, :]
    per_token = jnp.sum(matches.astype(jnp.int32), axis=1)
    rank_table = jnp.cumsum(per_token, axis=0) - per_token
    slot_iota = jnp.arange(capacity, dtype=jnp.int32)
    select = (per_token.T[:, None, :] == 1) & (rank_table.T[:, None, :] == slot_iota[None, :, None])
    return (matches.astype(jnp.float32), select)


def per_device(grad_out, top_logits, expert_ids, saved_hidden, w_down):
    count_experts = lax.axis_size("exp")
    slot_count = saved_hidden.shape[2]
    capacity = slot_count // count_experts
    model_width = grad_out.shape[1]
    onehot, select = routing_tables(expert_ids, count_experts, capacity)
    select_wide = select.astype(jnp.float32)
    gate_probs = jax.nn.softmax(top_logits, axis=-1)
    gate_sent = gate_probs.astype(jnp.bfloat16)
    gate_by_expert = jnp.sum(onehot * gate_sent.astype(jnp.float32)[:, :, None], axis=1)
    send_rows = jnp.einsum(
        "ect,td->ecd", select.astype(jnp.bfloat16), grad_out, preferred_element_type=jnp.float32
    ).astype(jnp.bfloat16)
    send_gate = jnp.sum(select_wide * gate_by_expert.T[:, None, :], axis=2).astype(jnp.bfloat16)
    hidden = saved_hidden[0, 0]
    rows_in, gate_in = (
        lax.all_to_all(send_rows, "exp", split_axis=0, concat_axis=0, tiled=True),
        lax.all_to_all(send_gate, "exp", split_axis=0, concat_axis=0, tiled=True),
    )
    flat_rows = rows_in.reshape(slot_count, model_width)
    backprop = lax.dot_general(
        flat_rows,
        lax.all_gather(w_down[0], "ctx", axis=0, tiled=True),
        (((1,), (1,)), ((), ())),
        preferred_element_type=jnp.float32,
    )
    flat_gate = gate_in.reshape(slot_count, 1).astype(jnp.float32)
    hidden_grad = (flat_gate * backprop).astype(jnp.bfloat16)
    slot_grad = jnp.sum(hidden.astype(jnp.float32) * backprop, axis=1)
    scaled = (flat_gate * flat_rows.astype(jnp.float32)).astype(jnp.bfloat16)
    partial_grad = lax.dot_general(
        hidden, scaled, (((0,), (0,)), ((), ())), preferred_element_type=jnp.float32
    )
    weight_grad = lax.psum_scatter(partial_grad, "ctx", scatter_dimension=0, tiled=True)
    returned = lax.all_to_all(
        slot_grad.reshape(count_experts, capacity), "exp", split_axis=0, concat_axis=0, tiled=True
    )
    grad_by_expert = jnp.sum(select_wide * returned[:, :, None], axis=1)
    gate_grad = jnp.sum(onehot * grad_by_expert.T[:, None, :], axis=2)
    logit_grad = gate_probs * (gate_grad - jnp.sum(gate_probs * gate_grad, axis=1, keepdims=True))
    return (logit_grad, hidden_grad.reshape(1, 1, slot_count, -1), weight_grad[None])


def solution(mesh):
    return jax.shard_map(
        per_device,
        mesh=mesh,
        in_specs=(
            P(("ctx", "exp"), None),
            P(("ctx", "exp"), None),
            P(("ctx", "exp"), None),
            P("ctx", "exp", None, None),
            P("exp", "ctx", None),
        ),
        out_specs=(P(("ctx", "exp"), None), P("ctx", "exp", None, None), P("exp", "ctx", None)),
        check_vma=False,
    )
```

profile of v0, /device:TPU:8, one launch (start us, length us, event | category | flops | bytes accessed | tf_op | source)
XLA Modules:
  0.0 434.2 jit_solution(5677177740942893195)
XLA Ops:
  7.2 0.0 copy-start
  7.2 0.0 all-gather.3.cloned.1.call-start
  7.2 0.7 all-gather.3.cloned.1.call-update
  7.9 0.7 convert_reduce_fusion
  8.6 0.1 copy.26
  8.7 0.2 reduce_window_sum.11
  8.9 0.0 copy-done
  9.0 3.4 convolution_convert_fusion
  12.4 0.0 copy-start.2
  12.4 0.0 copy-start.4
  12.4 6.8 %all-to-all-start = ((bf16[8,96,2880]{2,1,0:T(8,128)(2,1)}), bf16[8,96,2880]{2,1,0:T(8,128)(2,1)}, u32[]{:S(2)}, u32[]{:S(2)}) async-start(bf16[8,96,2880]{2,1,0:T(8,128)(2,1)} %convolution_convert_fusion), calls=%async_computation | async-start | bytes 9043968 | tf_op jit(solution)/shard_map/all_to_all | solution.py:33
  19.2 0.0 copy-done.2
  19.2 51.8 %all-to-all-done = bf16[8,96,2880]{2,1,0:T(8,128)(2,1)} async-done(((bf16[8,96,2880]{2,1,0:T(8,128)(2,1)}), bf16[8,96,2880]{2,1,0:T(8,128)(2,1)}, u32[]{:S(2)}, u32[]{:S(2)}) %all-to-all-start) | async-done | bytes 4423712 | tf_op jit(solution)/shard_map/all_to_all | solution.py:33
  71.0 43.6 %all-gather.3.cloned.1.call-done = bf16[1,1536,2880]{2,1,0:T(8,128)(2,1)} async-done(((bf16[1,48,2880]{2,1,0:T(8,128)(2,1)}), bf16[1,1536,2880]{2,1,0:T(8,128)(2,1)}) %all-gather.3.cloned.1.call-update) | async-done | bytes 8847376 | tf_op jit(solution)/shard_map/all_gather | solution.py:39
  114.7 0.0 copy-done.4
  114.7 0.0 copy-start.3
  114.7 13.1 %multiply_reduce_fusion = (f32[768]{0:T(1024)S(1)}, f32[768,1536]{1,0:T(8,128)}) fusion(bf16[1,1,768,1536]{3,2,1,0:T(8,128)(2,1)S(1)} %copy-done.4, bf16[768,2880]{1,0:T(8,128)(2,1)} %bitcast.4, bf16[1,1536,2880]{2,1,0:T(8,128)(2,1)} %all-gather.3.cloned.1.call-done), kind=kOutput, calls=%fused_computation.6 | convolution fusion | flops 6798310400 | bytes 20352000 | tf_op jit(solution)/shard_map/dot_general | solution.py:37
  127.8 0.7 all_to_all.14
  128.4 4.8 %all-to-all-start.1 = ((f32[8,1,96]{2,1,0:T(1,128)}), f32[8,1,96]{2,1,0:T(1,128)S(1)}, u32[]{:S(2)}, u32[]{:S(2)}) async-start(f32[8,1,96]{2,1,0:T(1,128)} %all_to_all.14), calls=%async_computation.1 | async-start | bytes 8192 | tf_op jit(solution)/shard_map/all_to_all | solution.py:51
  133.3 0.0 reduce-scatter.4.cloned.1.call-start
  133.3 0.0 copy-done.3
  133.3 3.7 all-to-all-done.1
  137.0 0.4 select_reduce_fusion
  137.4 7.7 %all_to_all.20 = bf16[8,1,96]{2,1,0:T(2,128)(2,1)S(1)} all-to-all(bf16[8,1,96]{2,1,0:T(2,128)(2,1)S(1)} %copy.29), channel_id=1, replica_groups=mesh['ctx'=32,'exp'=8] {'exp'}, dimensions={0} | all-to-all | bytes 3072 | tf_op jit(solution)/shard_map/all_to_all | solution.py:34
  145.1 3.7 multiply_convert_fusion
  148.8 10.4 %convolution_bitcast_fusion = f32[1536,2880]{0,1:T(8,128)} fusion(bf16[768,2880]{1,0:T(8,128)(2,1)S(1)} %bitcast.34, bf16[1,1,768,1536]{3,2,1,0:T(8,128)(2,1)S(1)} %copy-done.4), kind=kOutput, calls=%fused_computation | convolution fusion | flops 6794772480 | bytes 24477696 | tf_op jit(solution)/shard_map/dot_general | solution.py:47
  159.1 18.1 %copy.31 = f32[1536,2880]{1,0:T(8,128)} copy(f32[1536,2880]{0,1:T(8,128)} %convolution_bitcast_fusion) | data formatting | bytes 35389440
  177.2 0.0 reduce-scatter.4.cloned.1.call-update
  177.3 0.6 subtract_multiply_fusion
  177.9 0.1 reshape.60
  178.0 0.0 copy-start.1
  178.0 4.1 fusion.2
  182.1 242.5 %reduce-scatter.4.cloned.1.call-done = f32[48,2880]{1,0:T(8,128)} async-done(((f32[1536,2880]{1,0:T(8,128)}), f32[48,2880]{1,0:T(8,128)}) %reduce-scatter.4.cloned.1.call-update) | async-done | bytes 552976
  424.6 1.5 copy.32
  426.1 1.3 copy.30
  427.4 0.0 copy-done.1
  (12 shorter events, 0.2 us)
Async XLA Ops:
  7.2 1.8 copy-start
  7.2 107.5 %all-gather.3.cloned.1.call-start = ((), (), s32[]{:S(2)}) async-start(), calls=%async_computation.4 | async-start | bytes 9326592 | tf_op jit(solution)/shard_map/all_gather | solution.py:39
  12.4 6.8 %copy-start.2 = (f32[128,4]{0,1:T(4,128)S(1)}, f32[128,4]{0,1:T(4,128)}, u32[]{:S(2)}) copy-start(f32[128,4]{0,1:T(4,128)} %param.6) | copy-start | bytes 6148
  12.4 102.3 %copy-start.4 = (bf16[1,1,768,1536]{3,2,1,0:T(8,128)(2,1)S(1)}, bf16[1,1,768,1536]{3,2,1,0:T(8,128)(2,1)}, u32[]{:S(2)}) copy-start(bf16[1,1,768,1536]{3,2,1,0:T(8,128)(2,1)} %param.8) | copy-start | bytes 7077892
  12.4 58.6 %all-to-all-start = ((bf16[8,96,2880]{2,1,0:T(8,128)(2,1)}), bf16[8,96,2880]{2,1,0:T(8,128)(2,1)}, u32[]{:S(2)}, u32[]{:S(2)}) async-start(bf16[8,96,2880]{2,1,0:T(8,128)(2,1)} %convolution_convert_fusion), calls=%async_computation | async-start | bytes 9043968 | tf_op jit(solution)/shard_map/all_to_all | solution.py:33
  114.7 18.6 %copy-start.3 = (s32[128,4]{0,1:T(4,128)S(1)}, s32[128,4]{0,1:T(4,128)}, u32[]{:S(2)}) copy-start(s32[128,4]{0,1:T(4,128)} %param.7) | copy-start | bytes 6148
  128.4 8.6 %all-to-all-start.1 = ((f32[8,1,96]{2,1,0:T(1,128)}), f32[8,1,96]{2,1,0:T(1,128)S(1)}, u32[]{:S(2)}, u32[]{:S(2)}) async-start(f32[8,1,96]{2,1,0:T(1,128)} %all_to_all.14), calls=%async_computation.1 | async-start | bytes 8192 | tf_op jit(solution)/shard_map/all_to_all | solution.py:51
  133.3 291.3 %reduce-scatter.4.cloned.1.call-start = ((), (), s32[]{:S(2)}) async-start(), calls=%async_computation.5 | async-start | bytes 18653184
  178.0 249.4 %copy-start.1 = (bf16[128,2880]{0,1:T(8,128)(2,1)S(1)}, bf16[128,2880]{0,1:T(8,128)(2,1)}, u32[]{:S(2)}) copy-start(bf16[128,2880]{0,1:T(8,128)(2,1)} %param.5) | copy-start | bytes 2211844
Sparse Core Ops, SparseCore 0:
  10.6 104.0 all-gather.2
  177.4 247.1 reduce-scatter.3
where the time goes:
time: 435 us; the launch traced here: 434 us
  waiting for transfers between devices  342 us (79%)
  matrix products  26.9 us (6%)
  local copies, waits for them, and re-layouts  21.8 us (5%)
  between operations  14.1 us (3%)
  starting transfers between devices  11.7 us (3%)
  other arithmetic  9.78 us (2%)
  blocking collectives  7.66 us (2%)
    unnamed x3, waiting for transfers between devices  243 us
    all_to_all x1, waiting for transfers between devices, per_device(): lax.all_to_all(send_rows, 'exp', split_axis=0, concat_axis=0, tiled=True)  51.8 us
    all_gather x1, waiting for transfers between devices, per_device(): lax.all_gather(w_down[0], 'ctx', axis=0, tiled=True)  43.6 us
    unnamed x13, local copies, waits for them, and re-layouts  20.9 us
    dot_general x1, matrix products, per_device(): lax.dot_general(flat_rows, lax.all_gather(w_down[0], 'ctx', axis=0, tiled...  13.1 us
    dot_general x1, matrix products, per_device(): lax.dot_general(hidden, scaled, (((0,), (0,)), ((), ())), preferred_eleme...  10.4 us
  transfers between devices with their start and end apart: 4, of which 4 were waited for; matrix products, arithmetic and copies ran while one was open for 2% of the time, Pallas kernels for 0%

commit v1 on v0

--- a/solution.py
+++ b/solution.py
@@ -34,9 +34,17 @@
         lax.all_to_all(send_gate, "exp", split_axis=0, concat_axis=0, tiled=True),
     )
     flat_rows = rows_in.reshape(slot_count, model_width)
+
+    def space_return_all(inp, net_axis):
+        t_next = jnp.concatenate(
+            lax.all_to_all(jnp.stack(lax.axis_size(net_axis) * [inp], axis=0), net_axis, 0, 0),
+            axis=0,
+        )
+        return t_next
+
     backprop = lax.dot_general(
         flat_rows,
-        lax.all_gather(w_down[0], "ctx", axis=0, tiled=True),
+        space_return_all(w_down[0], "ctx"),
         (((1,), (1,)), ((), ())),
         preferred_element_type=jnp.float32,
     )

time: 435 us -> 618 us (1.42)
  waiting for transfers between devices: 342 us -> 462 us
  blocking collectives: 7.66 us -> 65.6 us
    all_to_all x1, waiting for transfers between devices: 51.8 us -> 203 us  [space_return_all(): lax.all_to_all(jnp.stack(lax.axis_size(net_axis) * [inp], axis=0), net_ax...]
    all_to_all x0 -> x1, blocking collectives: none -> 57.9 us  [per_device(): lax.all_to_all(send_rows, 'exp', split_axis=0, concat_axis=0, tiled=True)]
    all_gather x1 -> x0, waiting for transfers between devices: 43.6 us -> none  [per_device(): lax.all_gather(w_down[0], 'ctx', axis=0, tiled=True)]
    unnamed x3 -> x2, waiting for transfers between devices: 243 us -> 256 us
    unnamed x13 -> x15, local copies, waits for them, and re-layouts: 20.9 us -> 20.9 us
  transfers between devices with their start and end apart: 4 -> 3, of which waited for: 4 -> 3; matrix products, arithmetic and copies ran while one was open for 2% -> 1% of each run, Pallas kernels for 0% -> 0%
where the time goes in v1:
time: 618 us
  waiting for transfers between devices  462 us (75%)
  blocking collectives  65.6 us (11%)
  local copies, waits for them, and re-layouts  25.9 us (4%)
  matrix products  24.8 us (4%)
  starting transfers between devices  15 us (2%)
  between operations  14.1 us (2%)
  other arithmetic  9.86 us (2%)
    unnamed x2, waiting for transfers between devices  256 us
    all_to_all x1, waiting for transfers between devices, space_return_all(): lax.all_to_all(jnp.stack(lax.axis_size(net_axis) * [inp], axis=0), net_ax...  203 us
    all_to_all x1, blocking collectives, per_device(): lax.all_to_all(send_rows, 'exp', split_axis=0, concat_axis=0, tiled=True)  57.9 us
    unnamed x15, local copies, waits for them, and re-layouts  20.9 us
    dot_general x1, matrix products, per_device(): lax.dot_general(flat_rows, space_return_all(w_down[0], 'ctx'), (((1,), (1...  13.1 us
  transfers between devices with their start and end apart: 3, of which 3 were waited for; matrix products, arithmetic and copies ran while one was open for 1% of the time, Pallas kernels for 0%

profile of v1, /device:TPU:8, one launch (start us, length us, event | category | flops | bytes accessed | tf_op | source)
XLA Modules:
  0.0 617.6 jit_solution(8847469725952639819)
XLA Ops:
  7.2 0.0 copy-start
  7.2 0.8 convert_reduce_fusion
  8.0 0.1 copy.26
  8.1 0.2 reduce_window_sum.11
  8.3 0.0 copy-done
  8.3 1.3 convolution_convert_fusion
  9.7 0.0 copy-start.2
  9.7 57.9 %all_to_all.25 = bf16[8,96,2880]{2,1,0:T(8,128)(2,1)} all-to-all(bf16[8,96,2880]{2,1,0:T(8,128)(2,1)S(1)} %convolution_convert_fusion), channel_id=1, replica_groups=mesh['ctx'=32,'exp'=8] {'exp'}, dimensions={0} | all-to-all | bytes 8847360 | tf_op jit(solution)/shard_map/all_to_all | solution.py:33
  67.6 0.0 copy-done.2
  67.6 4.1 stack.3
  71.7 0.0 copy-start.3
  71.7 0.0 copy-start.5
  71.7 10.9 %all-to-all-start.1 = ((bf16[32,48,2880]{2,1,0:T(8,128)(2,1)}), bf16[32,48,2880]{2,1,0:T(8,128)(2,1)}, u32[]{:S(2)}, u32[]{:S(2)}) async-start(bf16[32,48,2880]{2,1,0:T(8,128)(2,1)} %stack.3), calls=%async_computation.1 | async-start | bytes 18087936 | tf_op jit(solution)/shard_map/all_to_all | solution.py:40
  82.6 0.0 copy-done.3
  82.7 202.9 %all-to-all-done.1 = bf16[32,48,2880]{2,1,0:T(8,128)(2,1)} async-done(((bf16[32,48,2880]{2,1,0:T(8,128)(2,1)}), bf16[32,48,2880]{2,1,0:T(8,128)(2,1)}, u32[]{:S(2)}, u32[]{:S(2)}) %all-to-all-start.1) | async-done | bytes 8847392 | tf_op jit(solution)/shard_map/all_to_all | solution.py:40
  285.6 0.0 copy-done.5
  285.6 0.0 copy-start.4
  285.6 13.1 %multiply_reduce_fusion = (f32[768]{0:T(1024)S(1)}, f32[768,1536]{1,0:T(8,128)}) fusion(bf16[1,1,768,1536]{3,2,1,0:T(8,128)(2,1)S(1)} %copy-done.5, bf16[768,2880]{1,0:T(8,128)(2,1)} %bitcast.31, bf16[1536,2880]{1,0:T(8,128)(2,1)} %bitcast.6), kind=kOutput, calls=%fused_computation.4 | convolution fusion | flops 6798310400 | bytes 20352000 | tf_op jit(solution)/shard_map/dot_general | solution.py:45
  298.7 0.7 all_to_all.18
  299.3 4.1 all-to-all-start.2
  303.4 0.0 reduce-scatter.4.cloned.1.call-start
  303.4 0.0 copy-done.4
  303.5 3.8 all-to-all-done.2
  307.2 0.4 select_reduce_fusion
  307.6 7.6 %all_to_all.26 = bf16[8,1,96]{2,1,0:T(2,128)(2,1)S(1)} all-to-all(bf16[8,1,96]{2,1,0:T(2,128)(2,1)S(1)} %copy.29), channel_id=1, replica_groups=mesh['ctx'=32,'exp'=8] {'exp'}, dimensions={0} | all-to-all | bytes 3072 | tf_op jit(solution)/shard_map/all_to_all | solution.py:34
  315.2 3.7 multiply_convert_fusion
  318.9 10.4 %convolution_bitcast_fusion = f32[1536,2880]{0,1:T(8,128)} fusion(bf16[768,2880]{1,0:T(8,128)(2,1)S(1)} %bitcast.33, bf16[1,1,768,1536]{3,2,1,0:T(8,128)(2,1)S(1)} %copy-done.5), kind=kOutput, calls=%fused_computation | convolution fusion | flops 6794772480 | bytes 24477696 | tf_op jit(solution)/shard_map/dot_general | solution.py:55
  329.3 18.1 %copy.31 = f32[1536,2880]{1,0:T(8,128)} copy(f32[1536,2880]{0,1:T(8,128)} %convolution_bitcast_fusion) | data formatting | bytes 35389440
  347.4 0.0 reduce-scatter.4.cloned.1.call-update
  347.5 0.6 subtract_multiply_fusion
  348.1 0.1 reshape.65
  348.2 0.0 copy-start.1
  348.2 4.1 fusion
  352.3 255.7 %reduce-scatter.4.cloned.1.call-done = f32[48,2880]{1,0:T(8,128)} async-done(((f32[1536,2880]{1,0:T(8,128)}), f32[48,2880]{1,0:T(8,128)}) %reduce-scatter.4.cloned.1.call-update) | async-done | bytes 552976
  608.0 1.5 copy.32
  609.5 1.3 copy.30
  610.8 0.0 copy-done.1
  (12 shorter events, 0.2 us)
Async XLA Ops:
  7.2 1.1 copy-start
  9.7 57.9 %copy-start.2 = (bf16[1,48,2880]{2,1,0:T(8,128)(2,1)S(1)}, bf16[1,48,2880]{2,1,0:T(8,128)(2,1)}, u32[]{:S(2)}) copy-start(bf16[1,48,2880]{2,1,0:T(8,128)(2,1)} %param.9) | copy-start | bytes 829444
  71.7 10.9 %copy-start.3 = (f32[128,4]{0,1:T(4,128)S(1)}, f32[128,4]{0,1:T(4,128)}, u32[]{:S(2)}) copy-start(f32[128,4]{0,1:T(4,128)} %param.6) | copy-start | bytes 6148
  71.7 213.9 %copy-start.5 = (bf16[1,1,768,1536]{3,2,1,0:T(8,128)(2,1)S(1)}, bf16[1,1,768,1536]{3,2,1,0:T(8,128)(2,1)}, u32[]{:S(2)}) copy-start(bf16[1,1,768,1536]{3,2,1,0:T(8,128)(2,1)} %param.8) | copy-start | bytes 7077892
  71.7 213.9 %all-to-all-start.1 = ((bf16[32,48,2880]{2,1,0:T(8,128)(2,1)}), bf16[32,48,2880]{2,1,0:T(8,128)(2,1)}, u32[]{:S(2)}, u32[]{:S(2)}) async-start(bf16[32,48,2880]{2,1,0:T(8,128)(2,1)} %stack.3), calls=%async_computation.1 | async-start | bytes 18087936 | tf_op jit(solution)/shard_map/all_to_all | solution.py:40
  285.6 17.9 %copy-start.4 = (s32[128,4]{0,1:T(4,128)S(1)}, s32[128,4]{0,1:T(4,128)}, u32[]{:S(2)}) copy-start(s32[128,4]{0,1:T(4,128)} %param.7) | copy-start | bytes 6148
  299.3 7.9 %all-to-all-start.2 = ((f32[8,1,96]{2,1,0:T(1,128)}), f32[8,1,96]{2,1,0:T(1,128)S(1)}, u32[]{:S(2)}, u32[]{:S(2)}) async-start(f32[8,1,96]{2,1,0:T(1,128)} %all_to_all.18), calls=%async_computation.2 | async-start | bytes 8192 | tf_op jit(solution)/shard_map/all_to_all | solution.py:59
  303.4 304.6 %reduce-scatter.4.cloned.1.call-start = ((), (), s32[]{:S(2)}) async-start(), calls=%async_computation.5 | async-start | bytes 18653184
  348.2 262.6 %copy-start.1 = (bf16[128,2880]{0,1:T(8,128)(2,1)S(1)}, bf16[128,2880]{0,1:T(8,128)(2,1)}, u32[]{:S(2)}) copy-start(bf16[128,2880]{0,1:T(8,128)(2,1)} %param.5) | copy-start | bytes 2211844
Sparse Core Ops, SparseCore 0:
  347.6 260.3 reduce-scatter.3
